TPU v7x, 32 devices: a whole 2x2x4 slice. The times are simulated.
32 devices in a mesh: dp: 4 (over z), ctx: 2 (over core), tp: 4 (over y, x).
Axes of the slice: x: 2, y: 2, z: 4, core: 2. Of those that a mesh axis runs over, the one named last changes fastest.
Arguments:
- block_in: bfloat16 [8192, 2048], P(('dp', 'ctx')), may hold values from -6 to 6
- query_proj: bfloat16 [2048, 2048], P('dp', 'tp'), may hold values from -0.125 to 0.125
- forget_proj: bfloat16 [2048, 2048], P('dp', 'tp'), may hold values from -0.0625 to 0.0625
- value_proj: bfloat16 [2048, 2048], P('dp', 'tp'), may hold values from -0.125 to 0.125
- outgate_proj: bfloat16 [2048, 2048], P('dp', 'tp'), may hold values from -0.125 to 0.125
- out_proj: bfloat16 [2048, 2048], P('tp', 'dp'), may hold values from -0.125 to 0.125
- ffn_gate: bfloat16 [2048, 5632], P('dp', 'tp'), may hold values from -0.125 to 0.125
- ffn_up: bfloat16 [2048, 5632], P('dp', 'tp'), may hold values from -0.125 to 0.125
- ffn_down: bfloat16 [5632, 2048], P('tp', 'dp'), may hold values from -0.078125 to 0.078125
- first_gain: float32 [2048], replicated, may hold values from 0.5 to 1.5
- second_gain: float32 [2048], replicated, may hold values from 0.5 to 1.5
- group_gain: float32 [2048], P('tp'), may hold values from 0.5 to 1.5
- forget_bias: float32 [2048], P('tp'), may hold values from 3 to 12
- bound_table: float32 [24, 2048], P(None, 'tp'), may hold values from -4 to 4
- layer_index: int32 [1], replicated, may hold values from 1 to 23
- second_start: int32 [4], P('dp'), may hold values from 1 to 2048, as said below
- cotangent: bfloat16 [8192, 2048], P(('dp', 'ctx')), may hold values from -6 to 6
Outputs:
- block_out: bfloat16 [8192, 2048], P(('dp', 'ctx'))
- input_grad: float32 [8192, 2048], P(('dp', 'ctx'))
- query_grad: float32 [2048, 2048], P('dp', 'tp')
- forget_grad: float32 [2048, 2048], P('dp', 'tp')
- value_grad: float32 [2048, 2048], P('dp', 'tp')
- outgate_grad: float32 [2048, 2048], P('dp', 'tp')
- out_proj_grad: float32 [2048, 2048], P('tp', 'dp')
- ffn_gate_grad: float32 [2048, 5632], P('dp', 'tp')
- ffn_up_grad: float32 [2048, 5632], P('dp', 'tp')
- ffn_down_grad: float32 [5632, 2048], P('tp', 'dp')
- first_gain_grad: float32 [2048], replicated
- second_gain_grad: float32 [2048], replicated
- group_gain_grad: float32 [2048], P('tp')
- forget_bias_grad: float32 [2048], P('tp')
- bound_table_grad: float32 [24, 2048], P(None, 'tp')
Inputs may be any that keep to these rules, and one draw needn't show every extreme that they name: second_start[p] is 2048 where pack p is one whole sequence, and otherwise the position inside the pack where its second sequence begins; pack 0 is always one whole sequence and pack 1 always holds two. layer_index names a row of bound_table other than the first.
All inputs are finite; a program needn't handle non-finite values.
Results may differ from a plain program's by a relative error of at most 0.018.
Values may be sent and summed in bfloat16 or wider, within the bound.
No kernel may reach another device: no remote copies, remote signals or barrier semaphores. Data moves between devices by JAX's collectives and lax.ppermute only.
A program may use at most 384 MiB of HBM per device.

v0:
```python
import jax
import jax.numpy as jnp
from jax import lax
from jax.sharding import PartitionSpec as P

HEAD = 128
BLOCK = 32
HIGH = lax.Precision.HIGHEST
EPS_NORM = 1e-06
EPS_GROUP = 1e-05


def carried_in(value, axis, join, neutral):
    count, mine = (lax.axis_size(axis), lax.axis_index(axis))
    pieces = jax.tree.map(lambda part: lax.all_gather(part, axis), value)
    total = jax.tree.map(
        lambda part, zero: jnp.full_like(part, 0) + jnp.asarray(zero, part.dtype), value, neutral
    )

    def hop(position, total):
        longer = join(total, jax.tree.map(lambda part: part[position], pieces))
        return jax.tree.map(lambda new, old: jnp.where(position < mine, new, old), longer, total)

    return lax.fori_loop(0, count - 1, hop, total)


def carried_in_2(array, axis, combine, identity):
    peers, index = (lax.axis_size(axis), lax.axis_index(axis))
    everything = jax.tree.map(
        lambda part, kind: lax.all_gather(part.astype(kind), axis),
        array,
        jax.tree.map(lambda a: jnp.bfloat16 if a.dtype == jnp.float32 else a.dtype, array),
    )
    start = jax.tree.map(
        lambda part, zero: jnp.broadcast_to(jnp.asarray(zero, part.dtype), part.shape),
        array,
        identity,
    )

    def hop(k, before):
        at = peers - 1 - k
        reached = at > index
        new = combine(
            before, jax.tree.map(lambda part, own: part[at].astype(own.dtype), everything, array)
        )
        return jax.tree.map(lambda a, b: jnp.where(reached, a, b), new, before)

    return lax.fori_loop(0, peers, hop, start)


def rms_norm(rows_in, gain_vec):
    return (
        rows_in
        * lax.rsqrt(jnp.mean(rows_in * rows_in, axis=-1, keepdims=True) + EPS_NORM)
        * gain_vec
    )


def head_norm(mixed, pre_gate, gain_vec, head_count):
    row_count = mixed.shape[0]
    grouped = mixed.reshape(row_count, head_count, -1)
    scaled = grouped * lax.rsqrt(jnp.mean(grouped * grouped, axis=-1, keepdims=True) + EPS_GROUP)
    return scaled.reshape(row_count, -1) * gain_vec * jax.nn.silu(pre_gate)


def lower_bound(bound_rows, which_layer):
    weights = jax.nn.softmax(bound_rows, axis=0)
    rising = jnp.cumsum(weights, axis=0) - weights[0:1]
    picked = (
        lax.broadcasted_iota(jnp.int32, (bound_rows.shape[0], 1), 0) == which_layer[0]
    ).astype(bound_rows.dtype)
    return jnp.sum(rising * picked, axis=0)


def gate_values(pre_query, pre_forget, bias_vec, bound_vec):
    shifted = pre_forget + bias_vec
    forget = bound_vec + (1.0 - bound_vec) * jax.nn.sigmoid(shifted)
    return (jax.nn.silu(pre_query), (1.0 - bound_vec) * jax.nn.sigmoid(-shifted), jnp.log(forget))


def chain_link(earlier, later):
    return (earlier[0] * later[0], later[0][..., None] * earlier[1] + later[1])


def contract_last(left_side, right_side):
    return lax.dot_general(
        left_side, right_side, (((1,), (1,)), ((), ())), preferred_element_type=jnp.float32
    )


def contract_first(left_side, right_side):
    return lax.dot_general(
        left_side, right_side, (((0,), (0,)), ((), ())), preferred_element_type=jnp.float32
    )


def block_parts(queries, key_rows, values, log_forget, doc_ids, prev_doc, block_len):
    length, head_count, feature = queries.shape
    block_count = length // block_len
    blocked = (block_count, block_len, head_count, feature)
    queries = queries.reshape(blocked)
    key_rows = key_rows.reshape(blocked)
    values = values.reshape(blocked)
    decays = jnp.cumsum(log_forget.reshape(blocked), axis=1)
    doc_ids = doc_ids.reshape(block_count, block_len)
    before = jnp.concatenate([jnp.reshape(prev_doc, (1,)), doc_ids[:-1, block_len - 1]])
    middle = decays[:, block_len // 2 : block_len // 2 + 1]
    final_decay = decays[:, block_len - 1 :]
    scores = jnp.einsum(
        "nthc,nshc->nhts",
        queries * jnp.exp(decays - middle),
        key_rows * jnp.exp(middle - decays),
        precision=HIGH,
    )
    causal = lax.broadcasted_iota(jnp.int32, (block_len, block_len), 0) >= lax.broadcasted_iota(
        jnp.int32, (block_len, block_len), 1
    )
    allowed = causal[None] & (doc_ids[:, :, None] == doc_ids[:, None, :])
    scores = jnp.where(allowed[:, None], scores, 0.0)
    inside = jnp.einsum("nhts,nshe->nthe", scores, values, precision=HIGH)
    in_tail = (doc_ids == doc_ids[:, block_len - 1 :]).astype(decays.dtype)
    ending = key_rows * jnp.exp(final_decay - decays) * in_tail[:, :, None, None]
    states = jnp.einsum("nshc,nshe->nhce", ending, values, precision=HIGH)
    kept_flag = (doc_ids[:, block_len - 1] == before).astype(decays.dtype)
    carried = jnp.exp(final_decay[:, 0]) * kept_flag[:, None, None]
    entering = (doc_ids == before[:, None]).astype(decays.dtype)
    reached = queries * jnp.exp(decays) * entering[:, :, None, None]
    prefix_decay, prefix_state = lax.associative_scan(chain_link, (carried, states), axis=0)
    return (inside, reached, prefix_decay, prefix_state)


def finish(pieces, state_in):
    inside, reached, prefix_decay, prefix_state = pieces
    state_ends = prefix_decay[..., None] * state_in[None] + prefix_state
    state_starts = jnp.concatenate([state_in[None], state_ends[:-1]], axis=0)
    outside = jnp.einsum("nthc,nhce->nthe", reached, state_starts, precision=HIGH)
    summed = inside + outside
    block_count, block_len, head_count, feature = summed.shape
    return (summed.reshape(block_count * block_len, head_count, feature), state_ends[-1])


def body(
    block_in,
    query_proj,
    forget_proj,
    value_proj,
    outgate_proj,
    out_proj,
    ffn_gate,
    ffn_up,
    ffn_down,
    first_gain,
    second_gain,
    group_gain,
    forget_bias,
    bound_table,
    layer_index,
    second_start,
    cotangent,
):
    row_count = block_in.shape[0]
    local_width = query_proj.shape[1]
    head_count = local_width // HEAD
    hidden_width = ffn_gate.shape[1]
    inputs = block_in.astype(jnp.float32)
    first_low = rms_norm(inputs, first_gain).astype(jnp.bfloat16)
    mix_local = jnp.concatenate([query_proj, forget_proj, value_proj, outgate_proj], axis=1)
    ffn_local = jnp.concatenate([ffn_gate, ffn_up], axis=1)
    mix_full, out_full = (
        lax.all_gather(mix_local, "dp", axis=0, tiled=True),
        lax.all_gather(out_proj, "dp", axis=1, tiled=True),
    )
    projected = jnp.dot(first_low, mix_full, preferred_element_type=jnp.float32)
    pre_query = projected[:, :local_width]
    pre_forget = projected[:, local_width : 2 * local_width]
    pre_value = projected[:, 2 * local_width : 3 * local_width]
    pre_outgate = projected[:, 3 * local_width :]
    bound_vec = lower_bound(bound_table, layer_index)
    queries, key_rows, log_forget = gate_values(pre_query, pre_forget, forget_bias, bound_vec)
    offset = lax.axis_index("ctx") * row_count
    doc_ids = (offset + lax.iota(jnp.int32, row_count) >= second_start[0]).astype(jnp.int32)
    prev_doc = (offset - 1 >= second_start[0]).astype(jnp.int32)

    def to_heads(flat):
        return flat.reshape(row_count, head_count, HEAD)

    def mixer(queries_in, keys_in, values_in, logs_in, state_in):
        return finish(
            block_parts(queries_in, keys_in, values_in, logs_in, doc_ids, prev_doc, BLOCK), state_in
        )

    pieces = block_parts(
        to_heads(queries),
        to_heads(key_rows),
        to_heads(pre_value),
        to_heads(log_forget),
        doc_ids,
        prev_doc,
        BLOCK,
    )
    identity = (
        jnp.ones((head_count, HEAD), jnp.float32),
        jnp.zeros((head_count, HEAD, HEAD), jnp.float32),
    )
    shard_decay = pieces[2][-1]
    entry_pair = carried_in((shard_decay, pieces[3][-1]), "ctx", chain_link, identity)
    state_in = entry_pair[1]
    mixed, _ = finish(pieces, state_in)
    mixed_flat = mixed.reshape(row_count, local_width)
    gated_low = head_norm(mixed_flat, pre_outgate, group_gain, head_count).astype(jnp.bfloat16)
    mix_partial = jnp.dot(gated_low, out_full, preferred_element_type=jnp.float32)
    resid = inputs + lax.psum(mix_partial, "tp")
    second_low = rms_norm(resid, second_gain).astype(jnp.bfloat16)
    ffn_full, down_full = (
        lax.all_gather(ffn_local, "dp", axis=0, tiled=True),
        lax.all_gather(ffn_down, "dp", axis=1, tiled=True),
    )
    gate_up = jnp.dot(second_low, ffn_full, preferred_element_type=jnp.float32)
    pre_gate = gate_up[:, :hidden_width]
    pre_up = gate_up[:, hidden_width:]
    hidden_low = (jax.nn.silu(pre_gate) * pre_up).astype(jnp.bfloat16)
    ffn_partial = jnp.dot(hidden_low, down_full, preferred_element_type=jnp.float32)
    block_out = (
        resid + lax.psum(ffn_partial.astype(jnp.bfloat16), "tp").astype(jnp.float32)
    ).astype(jnp.bfloat16)
    mix_full, out_full, ffn_full, down_full = (
        lax.all_gather(mix_local, "dp", axis=0, tiled=True),
        lax.all_gather(out_proj, "dp", axis=1, tiled=True),
        lax.all_gather(ffn_local, "dp", axis=0, tiled=True),
        lax.all_gather(ffn_down, "dp", axis=1, tiled=True),
    )
    cotangent_full = cotangent.astype(jnp.float32)
    hidden_grad = contract_last(cotangent, down_full)
    down_weight_grad = contract_first(hidden_low, cotangent)
    _, act_pull = jax.vjp(lambda gate_in, up_in: jax.nn.silu(gate_in) * up_in, pre_gate, pre_up)
    gate_grad, up_grad = act_pull(hidden_grad)
    gate_up_grad = jnp.concatenate([gate_grad, up_grad], axis=1).astype(jnp.bfloat16)
    second_part = contract_last(gate_up_grad, ffn_full)
    ffn_weight_grad = contract_first(second_low, gate_up_grad)
    second_total = lax.psum(second_part, "tp")
    _, second_pull = jax.vjp(rms_norm, resid, second_gain)
    resid_part, second_gain_grad = second_pull(second_total)
    resid_grad = cotangent_full + resid_part
    resid_low = resid_grad.astype(jnp.bfloat16)
    gated_grad = contract_last(resid_low, out_full)
    out_weight_grad = contract_first(gated_low, resid_low)
    _, head_pull = jax.vjp(
        lambda mixed_in, gate_in, gain_in: head_norm(mixed_in, gate_in, gain_in, head_count),
        mixed_flat,
        pre_outgate,
        group_gain,
    )
    mixed_grad, outgate_pre_grad, group_gain_grad = head_pull(gated_grad)
    _, mixer_pull = jax.vjp(
        mixer,
        to_heads(queries),
        to_heads(key_rows),
        to_heads(pre_value),
        to_heads(log_forget),
        state_in,
    )
    first_pass = mixer_pull(
        (to_heads(mixed_grad), jnp.zeros((head_count, HEAD, HEAD), jnp.float32))
    )
    after_pair = carried_in_2((shard_decay, first_pass[4]), "ctx", chain_link, identity)
    second_pass = mixer_pull((jnp.zeros((row_count, head_count, HEAD), jnp.float32), after_pair[1]))
    query_rec_grad = (first_pass[0] + second_pass[0]).reshape(row_count, local_width)
    key_rec_grad = (first_pass[1] + second_pass[1]).reshape(row_count, local_width)
    value_rec_grad = (first_pass[2] + second_pass[2]).reshape(row_count, local_width)
    log_rec_grad = (first_pass[3] + second_pass[3]).reshape(row_count, local_width)
    _, gate_pull = jax.vjp(gate_values, pre_query, pre_forget, forget_bias, bound_vec)
    query_pre_grad, forget_pre_grad, forget_bias_grad, bound_grad = gate_pull(
        (query_rec_grad, key_rec_grad, log_rec_grad)
    )
    _, table_pull = jax.vjp(lambda rows_in: lower_bound(rows_in, layer_index), bound_table)
    (table_grad,) = table_pull(bound_grad)
    proj_grad = jnp.concatenate(
        [query_pre_grad, forget_pre_grad, value_rec_grad, outgate_pre_grad], axis=1
    ).astype(jnp.bfloat16)
    first_part = contract_last(proj_grad, mix_full)
    mix_weight_grad = contract_first(first_low, proj_grad)
    first_total = lax.psum(first_part.astype(jnp.bfloat16), "tp").astype(jnp.float32)
    _, first_pull = jax.vjp(rms_norm, inputs, first_gain)
    input_part, first_gain_grad = first_pull(first_total)
    input_grad = resid_grad + input_part
    mix_summed, out_summed, ffn_summed, down_summed = (
        lax.psum_scatter(
            mix_weight_grad.astype(jnp.bfloat16), ("dp", "ctx"), scatter_dimension=0, tiled=True
        ).astype(jnp.float32),
        lax.psum_scatter(
            out_weight_grad.astype(jnp.bfloat16), ("dp", "ctx"), scatter_dimension=1, tiled=True
        ).astype(jnp.float32),
        lax.psum_scatter(
            ffn_weight_grad.astype(jnp.bfloat16), ("dp", "ctx"), scatter_dimension=0, tiled=True
        ).astype(jnp.float32),
        lax.psum_scatter(
            down_weight_grad.astype(jnp.bfloat16), ("dp", "ctx"), scatter_dimension=1, tiled=True
        ).astype(jnp.float32),
    )
    mix_shard, out_shard, ffn_shard, down_shard = (
        lax.all_gather(mix_summed.astype(jnp.bfloat16), "ctx", axis=0, tiled=True).astype(
            mix_summed.dtype
        ),
        lax.all_gather(out_summed.astype(jnp.bfloat16), "ctx", axis=1, tiled=True).astype(
            out_summed.dtype
        ),
        lax.all_gather(ffn_summed.astype(jnp.bfloat16), "ctx", axis=0, tiled=True).astype(
            ffn_summed.dtype
        ),
        lax.all_gather(down_summed.astype(jnp.bfloat16), "ctx", axis=1, tiled=True).astype(
            down_summed.dtype
        ),
    )
    first_sum, second_sum, group_sum, bias_sum, table_sum = (
        lax.psum(first_gain_grad.astype(jnp.bfloat16), ("dp", "ctx")).astype(jnp.float32),
        lax.psum(second_gain_grad.astype(jnp.bfloat16), ("dp", "ctx")).astype(jnp.float32),
        lax.psum(group_gain_grad.astype(jnp.bfloat16), ("dp", "ctx")).astype(jnp.float32),
        lax.psum(forget_bias_grad.astype(jnp.bfloat16), ("dp", "ctx")).astype(jnp.float32),
        lax.psum(table_grad.astype(jnp.bfloat16), ("dp", "ctx")).astype(jnp.float32),
    )
    return (
        block_out,
        input_grad,
        mix_shard[:, :local_width],
        mix_shard[:, local_width : 2 * local_width],
        mix_shard[:, 2 * local_width : 3 * local_width],
        mix_shard[:, 3 * local_width :],
        out_shard,
        ffn_shard[:, :hidden_width],
        ffn_shard[:, hidden_width:],
        down_shard,
        first_sum,
        second_sum,
        group_sum,
        bias_sum,
        table_sum,
    )


def solution(mesh):
    return jax.shard_map(
        body,
        mesh=mesh,
        in_specs=(
            P(("dp", "ctx"), None),
            P("dp", "tp"),
            P("dp", "tp"),
            P("dp", "tp"),
            P("dp", "tp"),
            P("tp", "dp"),
            P("dp", "tp"),
            P("dp", "tp"),
            P("tp", "dp"),
            P(),
            P(),
            P("tp"),
            P("tp"),
            P(None, "tp"),
            P(),
            P("dp"),
            P(("dp", "ctx"), None),
        ),
        out_specs=(
            P(("dp", "ctx"), None),
            P(("dp", "ctx"), None),
            P("dp", "tp"),
            P("dp", "tp"),
            P("dp", "tp"),
            P("dp", "tp"),
            P("tp", "dp"),
            P("dp", "tp"),
            P("dp", "tp"),
            P("tp", "dp"),
            P(),
            P(),
            P("tp"),
            P("tp"),
            P(None, "tp"),
        ),
        check_vma=False,
    )
```

profile of v0, /device:TPU:0, one launch (start us, length us, event | category | flops | bytes accessed | tf_op | source)
XLA Modules:
  0.0 2218.8 jit_solution(17821822070272523341)
XLA Ops:
  17.0 145.9 %all-gather.8.cloned.1.call-done = bf16[2048,2048]{1,0:T(8,128)(2,1)} async-done(((bf16[512,2048]{1,0:T(8,128)(2,1)}), bf16[2048,2048]{1,0:T(8,128)(2,1)}) %all-gather.8.cloned.1.call-update) | async-done | bytes 8388624 | tf_op jit(solution)/shard_map/all_gather | solution.py:170
  268.4 18.6 pad.557
  312.1 35.5 %pad.734 = f32[31,4,128,128]{2,3,1,0:T(8,128)} pad(f32[16,4,128,128]{2,3,1,0:T(8,128)} %pad_maximum_fusion.5, f32[]{:T(128)} %constant.113.clone.1), padding=0_0_1x0_0_0x0_0_0x0_0_0 | pad | bytes 12320772 | tf_op jit(solution)/shard_map/slice | solution.py:135
  347.6 35.6 %pad.559 = f32[32,4,128,128]{2,3,1,0:T(8,128)} pad(f32[16,4,128,128]{2,3,1,0:T(8,128)} %pad_maximum_fusion.5, f32[]{:T(128)} %constant.113.clone.1), padding=0_1_1x0_0_0x0_0_0x0_0_0 | pad | bytes 12582916 | tf_op jit(solution)/shard_map/pad | solution.py:128
  385.0 35.6 %pad.1005 = f32[32,4,128,128]{2,3,1,0:T(8,128)} pad(f32[16,4,128,128]{2,3,1,0:T(8,128)} %add.591, f32[]{:T(128)} %constant.113.clone.1), padding=1_0_1x0_0_0x0_0_0x0_0_0 | pad | bytes 12582916
  499.8 166.2 %all-reduce.122.cloned.1.call-done = f32[1024,2048]{1,0:T(8,128)} async-done(((f32[1024,2048]{1,0:T(8,128)}), f32[1024,2048]{1,0:T(8,128)}) %all-reduce.122.cloned.1.call-update) | async-done | bytes 8388624 | tf_op jit(solution)/shard_map/psum | solution.py:212
  675.0 194.9 %all-gather.12.cloned.1.call-done = bf16[2048,2816]{1,0:T(8,128)(2,1)} async-done(((bf16[512,2816]{1,0:T(8,128)(2,1)}), bf16[2048,2816]{1,0:T(8,128)(2,1)}) %all-gather.12.cloned.1.call-update) | async-done | bytes 11534352 | tf_op jit(solution)/shard_map/all_gather | solution.py:215
  869.9 20.0 fusion.177
  889.9 86.4 %all-gather.14.cloned.1.call-done = bf16[1408,2048]{1,0:T(8,128)(2,1)} async-done(((bf16[1408,512]{1,0:T(8,128)(2,1)}), bf16[1408,2048]{1,0:T(8,128)(2,1)}) %all-gather.14.cloned.1.call-update) | async-done | bytes 5767184 | tf_op jit(solution)/shard_map/all_gather | solution.py:216
  995.1 16.8 fusion.20
  1054.8 18.7 convolution_convert_fusion
  1084.6 97.8 %all-reduce.124.cloned.1.call-done = f32[1024,2048]{1,0:T(8,128)} async-done(((f32[1024,2048]{1,0:T(8,128)}), f32[1024,2048]{1,0:T(8,128)}) %all-reduce.124.cloned.1.call-update) | async-done | bytes 8388624 | tf_op jit(solution)/shard_map/psum | solution.py:240
  1413.1 18.5 pad.623
  1435.8 18.6 pad.624
  1510.5 35.6 %pad.625 = f32[32,4,128,128]{2,3,1,0:T(8,128)} pad(f32[16,4,128,128]{2,3,1,0:T(8,128)} %get-tuple-element.256, f32[]{:T(128)} %constant.113.clone.1), padding=1_0_1x0_0_0x0_0_0x0_0_0 | pad | bytes 12582916 | tf_op jit(solution)/shard_map/transpose(jvp())/pad | solution.py:128
  1546.0 35.5 %pad.591 = f32[32,4,128,128]{2,3,1,0:T(8,128)} pad(f32[16,4,128,128]{2,3,1,0:T(8,128)} %get-tuple-element.255, f32[]{:T(128)} %constant.113.clone.1), padding=1_0_1x0_0_0x0_0_0x0_0_0 | pad | bytes 12582916 | tf_op jit(solution)/shard_map/transpose(jvp())/pad | solution.py:128
  1590.3 35.6 %pad.592 = f32[32,4,128,128]{2,3,1,0:T(8,128)} pad(f32[16,4,128,128]{2,3,1,0:T(8,128)} %get-tuple-element.375, f32[]{:T(128)} %constant.113.clone.1), padding=0_1_1x0_0_0x0_0_0x0_0_0 | pad | bytes 12582916 | tf_op jit(solution)/shard_map/transpose(jvp())/pad | solution.py:128
  1625.9 35.7 %pad.626 = f32[32,4,128,128]{2,3,1,0:T(8,128)} pad(f32[16,4,128,128]{2,3,1,0:T(8,128)} %get-tuple-element.376, f32[]{:T(128)} %constant.113.clone.1), padding=0_1_1x0_0_0x0_0_0x0_0_0 | pad | bytes 12582916 | tf_op jit(solution)/shard_map/transpose(jvp())/pad | solution.py:128
  1661.7 33.6 %pad.562 = f32[32,4,128,128]{2,3,1,0:T(8,128)} pad(f32[15,4,128,128]{2,3,1,0:T(8,128)} %get-tuple-element.290, f32[]{:T(128)} %constant.113.clone.1), padding=2_1_1x0_0_0x0_0_0x0_0_0 | pad | bytes 12320772 | tf_op jit(solution)/shard_map/transpose(jvp())/pad | solution.py:128
  1695.3 33.7 %pad.597 = f32[32,4,128,128]{2,3,1,0:T(8,128)} pad(f32[15,4,128,128]{2,3,1,0:T(8,128)} %get-tuple-element.291, f32[]{:T(128)} %constant.113.clone.1), padding=2_1_1x0_0_0x0_0_0x0_0_0 | pad | bytes 12320772 | tf_op jit(solution)/shard_map/transpose(jvp())/pad | solution.py:128
  1810.3 19.3 fusion.176
  1913.4 152.0 %all-reduce.126.cloned.1.call-done = (bf16[1024,2048]{1,0:T(8,128)(2,1)}, bf16[1024,2048]{1,0:T(8,128)(2,1)}) async-done(((bf16[1024,2048]{1,0:T(8,128)(2,1)}, bf16[1024,2048]{1,0:T(8,128)(2,1)}), (bf16[1024,2048]{1,0:T(8,128)(2,1)}, bf16[1024,2048]{1,0:T(8,128)(2,1)})) %all-reduce.126.cloned.1.call-update) | async-done | bytes 8388624 | tf_op jit(solution)/shard_map/psum | solution.py:224
  2073.8 84.8 %reduce-scatter.5.cloned.1.call-done = bf16[256,2048]{1,0:T(8,128)(2,1)} async-done(((bf16[2048,2048]{1,0:T(8,128)(2,1)}), bf16[256,2048]{1,0:T(8,128)(2,1)}) %reduce-scatter.5.cloned.1.call-update) | async-done | bytes 1048592 | tf_op jit(solution)/shard_map/reduce_scatter | solution.py:287
  2164.6 26.3 %all-reduce.116 = (bf16[2048]{0:T(1024)(128)(2,1)S(1)}, bf16[2048]{0:T(1024)(128)(2,1)S(1)}, bf16[512]{0:T(512)(128)(2,1)S(1)}, bf16[512]{0:T(512)(128)(2,1)S(1)}, bf16[24,512]{1,0:T(8,128)(2,1)S(1)}) all-reduce(bf16[2048]{0:T(1024)(128)(2,1)S(1)} %get-tuple-element.200, ...), channel_id=1, replica_groups=mesh['dp'=4,'ctx'=2,'tp'=4] {'dp','ctx'}, use_global_device_ids=true, to_apply=%region_51.52 | all-reduce | flops 17408 | bytes 69632 | tf_op jit(solution)/shard_map/psum | solution.py:315
  (832 shorter events, 799.1 us)
Async XLA Ops:
  7.2 155.7 %all-gather.8.cloned.1.call-start = ((), (), s32[]{:S(2)}) async-start(), calls=%async_computation.4 | async-start | bytes 10485760 | tf_op jit(solution)/shard_map/all_gather | solution.py:170
  10.4 477.5 %all-gather.10.cloned.1.call-start = ((), (), s32[]{:S(2)}) async-start(), calls=%async_computation.5 | async-start | bytes 2621440 | tf_op jit(solution)/shard_map/all_gather | solution.py:171
  11.1 654.9 %all-reduce.122.cloned.1.call-start = ((), (), s32[]{:S(2)}) async-start(), calls=%async_computation.6 | async-start | bytes 16777216 | tf_op jit(solution)/shard_map/psum | solution.py:212
  16.4 159.0 %copy-start.171 = (f32[1024]{0:T(1024)}, f32[1024]{0:T(1024)S(1)}, u32[]{:S(2)}) copy-start(f32[1024]{0:T(1024)S(1)} %fusion.149) | copy-start | bytes 12292
  16.6 158.8 %copy-start.178 = (f32[512]{0:T(512)}, f32[512]{0:T(512)S(1)}, u32[]{:S(2)}) copy-start(f32[512]{0:T(512)S(1)} %multiply_reduce_fusion.28) | copy-start | bytes 6148
  16.6 158.8 %copy-start.196 = (f32[512]{0:T(512)}, f32[512]{0:T(512)S(1)}, u32[]{:S(2)}) copy-start(f32[512]{0:T(512)S(1)} %broadcast_subtract_fusion) | copy-start | bytes 6148
  16.7 169.4 %copy-start.214 = (f32[32]{0:T(128)}, f32[32]{0:T(128)S(1)}, u32[]{:S(2)}) copy-start(f32[32]{0:T(128)S(1)} %get-tuple-element.269) | copy-start | bytes 388
  16.9 1024.1 %copy-start.73 = (pred[32,32,32]{2,1,0:T(8,128)(4,1)}, pred[32,32,32]{2,1,0:T(8,128)(4,1)S(1)}, u32[]{:S(2)}) copy-start(pred[32,32,32]{2,1,0:T(8,128)(4,1)S(1)} %compare_and_fusion) | copy-start | bytes 98308
  16.9 189.3 %copy-start.131 = (f32[32,32]{0,1:T(8,128)}, f32[32,32]{0,1:T(8,128)S(1)}, u32[]{:S(2)}) copy-start(f32[32,32]{0,1:T(8,128)S(1)} %get-tuple-element.440) | copy-start | bytes 12292
  16.9 415.8 %copy-start.129 = (f32[32,32]{0,1:T(8,128)}, f32[32,32]{0,1:T(8,128)S(1)}, u32[]{:S(2)}) copy-start(f32[32,32]{0,1:T(8,128)S(1)} %get-tuple-element.439) | copy-start | bytes 12292
  17.0 158.5 %copy-start.204 = (f32[512]{0:T(512)S(1)}, f32[512]{0:T(512)}, u32[]{:S(2)}) copy-start(f32[512]{0:T(512)} %param.31) | copy-start | bytes 6148
  424.2 600.7 %copy-start.88 = (f32[1,4,128,128]{2,3,1,0:T(8,128)}, f32[1,4,128,128]{2,3,1,0:T(8,128)S(1)}, u32[]{:S(2)}) copy-start(f32[1,4,128,128]{2,3,1,0:T(8,128)S(1)} %add_select_fusion) | copy-start | bytes 786436
  495.5 374.3 %all-gather.12.cloned.1.call-start = ((), (), s32[]{:S(2)}) async-start(), calls=%async_computation.7 | async-start | bytes 14417920 | tf_op jit(solution)/shard_map/all_gather | solution.py:215
  499.2 477.1 %all-gather.14.cloned.1.call-start = ((), (), s32[]{:S(2)}) async-start(), calls=%async_computation.8 | async-start | bytes 7208960 | tf_op jit(solution)/shard_map/all_gather | solution.py:216
  499.7 370.1 %copy-start.177 = (f32[2048]{0:T(1024)S(1)}, f32[2048]{0:T(1024)}, u32[]{:S(2)}) copy-start(f32[2048]{0:T(1024)} %param.29) | copy-start | bytes 24580
  499.8 682.7 %all-reduce.124.cloned.1.call-start = ((), (), s32[]{:S(2)}) async-start(), calls=%async_computation.9 | async-start | bytes 16777216 | tf_op jit(solution)/shard_map/psum | solution.py:240
  1011.9 865.1 %reduce-scatter.11.cloned.1.call-start = ((), (), s32[]{:S(2)}) async-start(), calls=%async_computation.15 | async-start | bytes 6488064 | tf_op jit(solution)/shard_map/reduce_scatter | solution.py:296
  1022.5 882.9 %reduce-scatter.9.cloned.1.call-start = ((), (), s32[]{:S(2)}) async-start(), calls=%async_computation.13 | async-start | bytes 12976128 | tf_op jit(solution)/shard_map/reduce_scatter | solution.py:293
  1073.5 833.1 %reduce-scatter.7.cloned.1.call-start = ((), (), s32[]{:S(2)}) async-start(), calls=%async_computation.12 | async-start | bytes 2359296 | tf_op jit(solution)/shard_map/reduce_scatter | solution.py:290
  1808.8 101.3 %all-gather.20.cloned.1.call-start = ((), (), s32[]{:S(2)}) async-start(), calls=%async_computation.16 | async-start | bytes 2162688 | tf_op jit(solution)/shard_map/all_gather | solution.py:310
  1877.1 188.4 %all-reduce.126.cloned.1.call-start = ((), (), s32[]{:S(2)}) async-start(), calls=%async_computation.17 | async-start | bytes 16777216 | tf_op jit(solution)/shard_map/psum | solution.py:224
  1890.0 268.6 %reduce-scatter.5.cloned.1.call-start = ((), (), s32[]{:S(2)}) async-start(), calls=%async_computation.10 | async-start | bytes 9437184 | tf_op jit(solution)/shard_map/reduce_scatter | solution.py:287
  1905.3 298.1 %all-gather.18.cloned.1.call-start = ((), (), s32[]{:S(2)}) async-start(), calls=%async_computation.14 | async-start | bytes 4325376 | tf_op jit(solution)/shard_map/all_gather | solution.py:307
  1906.0 302.0 %all-gather.16.cloned.1.call-start = ((), (), s32[]{:S(2)}) async-start(), calls=%async_computation.11 | async-start | bytes 3145728 | tf_op jit(solution)/shard_map/all_gather | solution.py:301
  (237 other events, 2089.7 us)
Sparse Core Ops, SparseCore 0:
  10.5 152.3 all-gather.7
  164.4 44.1 all-gather.9
  495.6 170.3 all-reduce.121
  668.1 201.7 all-gather.11
  871.3 104.8 all-gather.13
  1012.0 170.3 all-reduce.123
  1184.7 65.5 reduce-scatter.10
  1252.6 117.6 reduce-scatter.8
  1808.8 36.2 reduce-scatter.6
  1877.2 10.0 all-gather.19
  1891.6 173.7 all-reduce.125
  2068.3 90.2 reduce-scatter.4
  2160.2 10.1 all-gather.17
  2171.8 11.7 all-gather.15
where the time goes:
time: 2250 us; the launch traced here: 2220 us
  waiting for transfers between devices  930 us (41%)
  local copies, waits for them, and re-layouts  640 us (28%)
  matrix products  319 us (14%)
  other arithmetic  275 us (12%)
  blocking collectives  36.4 us (2%)
    pad x74, local copies, waits for them, and re-layouts, block_parts(): lax.associative_scan(chain_link, (carried, states), axis=0)  483 us
    all_gather x1, waiting for transfers between devices, body(): lax.all_gather(ffn_local, 'dp', axis=0, tiled=True)  195 us
    psum x1, waiting for transfers between devices, body(): resid = inputs + lax.psum(mix_partial, 'tp')  166 us
    psum x1, waiting for transfers between devices, body(): lax.psum(ffn_partial.astype(jnp.bfloat16), 'tp').astype(jnp.float32)  152 us
    all_gather x1, waiting for transfers between devices, body(): lax.all_gather(mix_local, 'dp', axis=0, tiled=True)  146 us
    psum x1, waiting for transfers between devices, body(): second_total = lax.psum(second_part, 'tp')  97.8 us
    all_gather x1, waiting for transfers between devices, body(): lax.all_gather(ffn_down, 'dp', axis=1, tiled=True)  86.4 us
    reduce_scatter x1, waiting for transfers between devices, body(): lax.psum_scatter(mix_weight_grad.astype(jnp.bfloat16), ('dp', 'ctx'), sca...  84.8 us
  transfers between devices with their start and end apart: 14, of which 7 were waited for; matrix products, arithmetic and copies ran while one was open for 51% of the time, Pallas kernels for 0%

commit v1 on v0

--- a/solution.py
+++ b/solution.py
@@ -220,8 +220,11 @@
     pre_up = gate_up[:, hidden_width:]
     hidden_low = (jax.nn.silu(pre_gate) * pre_up).astype(jnp.bfloat16)
     ffn_partial = jnp.dot(hidden_low, down_full, preferred_element_type=jnp.float32)
+    find_digits = lambda x_part, shard_axis: jnp.sum(
+        lax.all_gather(x_part, axis_name=shard_axis), 0
+    )
     block_out = (
-        resid + lax.psum(ffn_partial.astype(jnp.bfloat16), "tp").astype(jnp.float32)
+        resid + find_digits(ffn_partial.astype(jnp.bfloat16), "tp").astype(jnp.float32)
     ).astype(jnp.bfloat16)
     mix_full, out_full, ffn_full, down_full = (
         lax.all_gather(mix_local, "dp", axis=0, tiled=True),

time: 2250 us -> 2530 us (1.12)
  waiting for transfers between devices: 930 us -> 1220 us
  local copies, waits for them, and re-layouts: 640 us -> 603 us
    all_gather x0 -> x1, waiting for transfers between devices: none -> 158 us  [body(): lax.all_gather(x_part, axis_name=shard_axis)]
    reduce_scatter x1, waiting for transfers between devices: 0.02 us -> 115 us  [body(): lax.psum_scatter(ffn_weight_grad.astype(jnp.bfloat16), ('dp', 'ctx'), sca...]
    psum x1, waiting for transfers between devices: 97.8 us -> 154 us  [body(): second_total = lax.psum(second_part, 'tp')]
    psum x1, waiting for transfers between devices: 152 us -> 102 us  [body(): lax.psum(first_part.astype(jnp.bfloat16), 'tp').astype(jnp.float32)]
    reduce_scatter x1, waiting for transfers between devices: 0.02 us -> 36.4 us  [body(): lax.psum_scatter(out_weight_grad.astype(jnp.bfloat16), ('dp', 'ctx'), sca...]
    pad x74, local copies, waits for them, and re-layouts: 483 us -> 455 us  [block_parts(): lax.associative_scan(chain_link, (carried, states), axis=0)]
    reduce_scatter x1, waiting for transfers between devices: 84.8 us -> 57.9 us  [body(): lax.psum_scatter(mix_weight_grad.astype(jnp.bfloat16), ('dp', 'ctx'), sca...]
    unnamed x468 -> x406, local copies, waits for them, and re-layouts: 79.2 us -> 70.8 us
  transfers between devices with their start and end apart: 14 -> 15, of which waited for: 7 -> 10; matrix products, arithmetic and copies ran while one was open for 51% -> 46% of each run, Pallas kernels for 0% -> 0%
where the time goes in v1:
time: 2530 us; the launch traced here: 2490 us
  waiting for transfers between devices  1220 us (48%)
  local copies, waits for them, and re-layouts  603 us (24%)
  matrix products  325 us (13%)
  other arithmetic  288 us (11%)
  blocking collectives  39 us (2%)
    pad x74, local copies, waits for them, and re-layouts, block_parts(): lax.associative_scan(chain_link, (carried, states), axis=0)  455 us
    all_gather x1, waiting for transfers between devices, body(): lax.all_gather(ffn_local, 'dp', axis=0, tiled=True)  195 us
    psum x1, waiting for transfers between devices, body(): resid = inputs + lax.psum(mix_partial, 'tp')  166 us
    all_gather x1, waiting for transfers between devices, body(): lax.all_gather(x_part, axis_name=shard_axis)  158 us
    psum x1, waiting for transfers between devices, body(): second_total = lax.psum(second_part, 'tp')  154 us
    all_gather x1, waiting for transfers between devices, body(): lax.all_gather(mix_local, 'dp', axis=0, tiled=True)  146 us
    reduce_scatter x1, waiting for transfers between devices, body(): lax.psum_scatter(ffn_weight_grad.astype(jnp.bfloat16), ('dp', 'ctx'), sca...  115 us
    psum x1, waiting for transfers between devices, body(): lax.psum(first_part.astype(jnp.bfloat16), 'tp').astype(jnp.float32)  102 us
  transfers between devices with their start and end apart: 15, of which 10 were waited for; matrix products, arithmetic and copies ran while one was open for 46% of the time, Pallas kernels for 0%

profile of v1, /device:TPU:0, one launch (start us, length us, event | category | flops | bytes accessed | tf_op | source)
XLA Modules:
  0.0 2493.0 jit_solution(4363003864523052526)
XLA Ops:
  17.0 145.9 %all-gather.10.cloned.1.call-done = bf16[2048,2048]{1,0:T(8,128)(2,1)} async-done(((bf16[512,2048]{1,0:T(8,128)(2,1)}), bf16[2048,2048]{1,0:T(8,128)(2,1)}) %all-gather.10.cloned.1.call-update) | async-done | bytes 8388624 | tf_op jit(solution)/shard_map/all_gather | solution.py:170
  312.0 35.4 %pad.734 = f32[31,4,128,128]{2,3,1,0:T(8,128)} pad(f32[16,4,128,128]{2,3,1,0:T(8,128)} %pad_maximum_fusion.5, f32[]{:T(128)} %constant.114.clone.1), padding=0_0_1x0_0_0x0_0_0x0_0_0 | pad | bytes 12320772 | tf_op jit(solution)/shard_map/slice | solution.py:135
  347.4 35.5 %pad.559 = f32[32,4,128,128]{2,3,1,0:T(8,128)} pad(f32[16,4,128,128]{2,3,1,0:T(8,128)} %pad_maximum_fusion.5, f32[]{:T(128)} %constant.114.clone.1), padding=0_1_1x0_0_0x0_0_0x0_0_0 | pad | bytes 12582916 | tf_op jit(solution)/shard_map/pad | solution.py:128
  384.7 35.6 %pad.1005 = f32[32,4,128,128]{2,3,1,0:T(8,128)} pad(f32[16,4,128,128]{2,3,1,0:T(8,128)} %add.589, f32[]{:T(128)} %constant.114.clone.1), padding=1_0_1x0_0_0x0_0_0x0_0_0 | pad | bytes 12582916
  499.1 166.2 %all-reduce.121.cloned.1.call-done = f32[1024,2048]{1,0:T(8,128)} async-done(((f32[1024,2048]{1,0:T(8,128)}), f32[1024,2048]{1,0:T(8,128)}) %all-reduce.121.cloned.1.call-update) | async-done | bytes 8388624 | tf_op jit(solution)/shard_map/psum | solution.py:212
  674.2 194.9 %all-gather.14.cloned.1.call-done = bf16[2048,2816]{1,0:T(8,128)(2,1)} async-done(((bf16[512,2816]{1,0:T(8,128)(2,1)}), bf16[2048,2816]{1,0:T(8,128)(2,1)}) %all-gather.14.cloned.1.call-update) | async-done | bytes 11534352 | tf_op jit(solution)/shard_map/all_gather | solution.py:215
  869.1 20.0 fusion.177
  889.1 86.4 %all-gather.16.cloned.1.call-done = bf16[1408,2048]{1,0:T(8,128)(2,1)} async-done(((bf16[1408,512]{1,0:T(8,128)(2,1)}), bf16[1408,2048]{1,0:T(8,128)(2,1)}) %all-gather.16.cloned.1.call-update) | async-done | bytes 5767184 | tf_op jit(solution)/shard_map/all_gather | solution.py:216
  1002.2 19.4 fusion.20
  1021.7 19.4 convolution_convert_fusion
  1085.8 154.1 %all-reduce.123.cloned.1.call-done = f32[1024,2048]{1,0:T(8,128)} async-done(((f32[1024,2048]{1,0:T(8,128)}), f32[1024,2048]{1,0:T(8,128)}) %all-reduce.123.cloned.1.call-update) | async-done | bytes 8388624 | tf_op jit(solution)/shard_map/psum | solution.py:243
  1247.5 114.7 %reduce-scatter.9.cloned.1.call-done = bf16[256,2816]{1,0:T(8,128)(2,1)} async-done(((bf16[2048,2816]{1,0:T(8,128)(2,1)}), bf16[256,2816]{1,0:T(8,128)(2,1)}) %reduce-scatter.9.cloned.1.call-update) | async-done | bytes 1441808 | tf_op jit(solution)/shard_map/reduce_scatter | solution.py:296
  1362.3 158.2 %all-gather.24.cloned.1.call-done = bf16[4096,2048]{1,0:T(8,128)(2,1)} async-done(((bf16[1024,2048]{1,0:T(8,128)(2,1)}), bf16[4096,2048]{1,0:T(8,128)(2,1)}) %all-gather.24.cloned.1.call-update) | async-done | bytes 16777232 | tf_op jit(solution)/shard_map/all_gather | solution.py:224
  1847.4 35.5 %pad.625 = f32[32,4,128,128]{2,3,1,0:T(8,128)} pad(f32[16,4,128,128]{2,3,1,0:T(8,128)} %get-tuple-element.254, f32[]{:T(128)} %constant.114.clone.1), padding=1_0_1x0_0_0x0_0_0x0_0_0 | pad | bytes 12582916 | tf_op jit(solution)/shard_map/transpose(jvp())/pad | solution.py:128
  1891.6 35.6 %pad.591 = f32[32,4,128,128]{2,3,1,0:T(8,128)} pad(f32[16,4,128,128]{2,3,1,0:T(8,128)} %get-tuple-element.253, f32[]{:T(128)} %constant.114.clone.1), padding=1_0_1x0_0_0x0_0_0x0_0_0 | pad | bytes 12582916 | tf_op jit(solution)/shard_map/transpose(jvp())/pad | solution.py:128
  1927.2 35.7 %pad.592 = f32[32,4,128,128]{2,3,1,0:T(8,128)} pad(f32[16,4,128,128]{2,3,1,0:T(8,128)} %get-tuple-element.375, f32[]{:T(128)} %constant.114.clone.1), padding=0_1_1x0_0_0x0_0_0x0_0_0 | pad | bytes 12582916 | tf_op jit(solution)/shard_map/transpose(jvp())/pad | solution.py:128
  1962.9 33.5 %pad.562 = f32[32,4,128,128]{2,3,1,0:T(8,128)} pad(f32[15,4,128,128]{2,3,1,0:T(8,128)} %get-tuple-element.290, f32[]{:T(128)} %constant.114.clone.1), padding=2_1_1x0_0_0x0_0_0x0_0_0 | pad | bytes 12320772 | tf_op jit(solution)/shard_map/transpose(jvp())/pad | solution.py:128
  2030.2 35.7 %pad.626 = f32[32,4,128,128]{2,3,1,0:T(8,128)} pad(f32[16,4,128,128]{2,3,1,0:T(8,128)} %get-tuple-element.376, f32[]{:T(128)} %constant.114.clone.1), padding=0_1_1x0_0_0x0_0_0x0_0_0 | pad | bytes 12582916 | tf_op jit(solution)/shard_map/transpose(jvp())/pad | solution.py:128
  2066.0 33.6 %pad.597 = f32[32,4,128,128]{2,3,1,0:T(8,128)} pad(f32[15,4,128,128]{2,3,1,0:T(8,128)} %get-tuple-element.291, f32[]{:T(128)} %constant.114.clone.1), padding=2_1_1x0_0_0x0_0_0x0_0_0 | pad | bytes 12320772 | tf_op jit(solution)/shard_map/transpose(jvp())/pad | solution.py:128
  2136.5 19.2 fusion.176
  2234.6 57.9 %reduce-scatter.5.cloned.1.call-done = bf16[256,2048]{1,0:T(8,128)(2,1)} async-done(((bf16[2048,2048]{1,0:T(8,128)(2,1)}), bf16[256,2048]{1,0:T(8,128)(2,1)}) %reduce-scatter.5.cloned.1.call-update) | async-done | bytes 1048592 | tf_op jit(solution)/shard_map/reduce_scatter | solution.py:290
  2292.6 36.4 %reduce-scatter.7.cloned.1.call-done = bf16[512,256]{1,0:T(8,128)(2,1)} async-done(((bf16[512,2048]{1,0:T(8,128)(2,1)}), bf16[512,256]{1,0:T(8,128)(2,1)}) %reduce-scatter.7.cloned.1.call-update) | async-done | bytes 262160 | tf_op jit(solution)/shard_map/reduce_scatter | solution.py:293
  2332.5 102.2 %all-reduce.125.cloned.1.call-done = bf16[1024,2048]{1,0:T(8,128)(2,1)} async-done(((bf16[1024,2048]{1,0:T(8,128)(2,1)}), bf16[1024,2048]{1,0:T(8,128)(2,1)}) %all-reduce.125.cloned.1.call-update) | async-done | bytes 4194320 | tf_op jit(solution)/shard_map/psum | solution.py:285
  2440.8 28.9 %all-reduce.116 = (bf16[2048]{0:T(1024)(128)(2,1)S(1)}, bf16[2048]{0:T(1024)(128)(2,1)S(1)}, bf16[512]{0:T(512)(128)(2,1)S(1)}, bf16[512]{0:T(512)(128)(2,1)S(1)}, bf16[24,512]{1,0:T(8,128)(2,1)S(1)}) all-reduce(bf16[2048]{0:T(1024)(128)(2,1)S(1)} %get-tuple-element.200, ...), channel_id=1, replica_groups=mesh['dp'=4,'ctx'=2,'tp'=4] {'dp','ctx'}, use_global_device_ids=true, to_apply=%region_51.52 | all-reduce | flops 17408 | bytes 69632 | tf_op jit(solution)/shard_map/psum | solution.py:318
  (764 shorter events, 834.8 us)
Async XLA Ops:
  7.2 155.7 %all-gather.10.cloned.1.call-start = ((), (), s32[]{:S(2)}) async-start(), calls=%async_computation.4 | async-start | bytes 10485760 | tf_op jit(solution)/shard_map/all_gather | solution.py:170
  10.4 476.8 %all-gather.12.cloned.1.call-start = ((), (), s32[]{:S(2)}) async-start(), calls=%async_computation.5 | async-start | bytes 2621440 | tf_op jit(solution)/shard_map/all_gather | solution.py:171
  11.1 654.2 %all-reduce.121.cloned.1.call-start = ((), (), s32[]{:S(2)}) async-start(), calls=%async_computation.6 | async-start | bytes 16777216 | tf_op jit(solution)/shard_map/psum | solution.py:212
  16.4 159.0 %copy-start.163 = (f32[1024]{0:T(1024)}, f32[1024]{0:T(1024)S(1)}, u32[]{:S(2)}) copy-start(f32[1024]{0:T(1024)S(1)} %fusion.149) | copy-start | bytes 12292
  16.6 158.8 %copy-start.165 = (f32[512]{0:T(512)}, f32[512]{0:T(512)S(1)}, u32[]{:S(2)}) copy-start(f32[512]{0:T(512)S(1)} %multiply_reduce_fusion.28) | copy-start | bytes 6148
  16.6 158.8 %copy-start.176 = (f32[512]{0:T(512)}, f32[512]{0:T(512)S(1)}, u32[]{:S(2)}) copy-start(f32[512]{0:T(512)S(1)} %broadcast_subtract_fusion) | copy-start | bytes 6148
  16.7 169.4 %copy-start.190 = (f32[32]{0:T(128)}, f32[32]{0:T(128)S(1)}, u32[]{:S(2)}) copy-start(f32[32]{0:T(128)S(1)} %get-tuple-element.267) | copy-start | bytes 388
  16.9 1563.9 %copy-start.69 = (pred[32,32,32]{2,1,0:T(8,128)(4,1)}, pred[32,32,32]{2,1,0:T(8,128)(4,1)S(1)}, u32[]{:S(2)}) copy-start(pred[32,32,32]{2,1,0:T(8,128)(4,1)S(1)} %compare_and_fusion) | copy-start | bytes 98308
  16.9 189.3 %copy-start.132 = (f32[32,32]{0,1:T(8,128)}, f32[32,32]{0,1:T(8,128)S(1)}, u32[]{:S(2)}) copy-start(f32[32,32]{0,1:T(8,128)S(1)} %get-tuple-element.440) | copy-start | bytes 12292
  16.9 415.5 %copy-start.130 = (f32[32,32]{0,1:T(8,128)}, f32[32,32]{0,1:T(8,128)S(1)}, u32[]{:S(2)}) copy-start(f32[32,32]{0,1:T(8,128)S(1)} %get-tuple-element.439) | copy-start | bytes 12292
  17.0 158.5 %copy-start.182 = (f32[512]{0:T(512)S(1)}, f32[512]{0:T(512)}, u32[]{:S(2)}) copy-start(f32[512]{0:T(512)} %param.31) | copy-start | bytes 6148
  494.8 374.3 %all-gather.14.cloned.1.call-start = ((), (), s32[]{:S(2)}) async-start(), calls=%async_computation.7 | async-start | bytes 14417920 | tf_op jit(solution)/shard_map/all_gather | solution.py:215
  498.4 477.1 %all-gather.16.cloned.1.call-start = ((), (), s32[]{:S(2)}) async-start(), calls=%async_computation.8 | async-start | bytes 7208960 | tf_op jit(solution)/shard_map/all_gather | solution.py:216
  499.0 370.1 %copy-start.175 = (f32[2048]{0:T(1024)S(1)}, f32[2048]{0:T(1024)}, u32[]{:S(2)}) copy-start(f32[2048]{0:T(1024)} %param.29) | copy-start | bytes 24580
  499.0 579.9 %reduce-scatter.11.cloned.1.call-start = ((), (), s32[]{:S(2)}) async-start(), calls=%async_computation.16 | async-start | bytes 6488064 | tf_op jit(solution)/shard_map/reduce_scatter | solution.py:299
  1002.1 237.7 %all-reduce.123.cloned.1.call-start = ((), (), s32[]{:S(2)}) async-start(), calls=%async_computation.9 | async-start | bytes 16777216 | tf_op jit(solution)/shard_map/psum | solution.py:243
  1021.7 340.6 %reduce-scatter.9.cloned.1.call-start = ((), (), s32[]{:S(2)}) async-start(), calls=%async_computation.14 | async-start | bytes 12976128 | tf_op jit(solution)/shard_map/reduce_scatter | solution.py:296
  1041.1 479.3 %all-gather.24.cloned.1.call-start = ((), (), s32[]{:S(2)}) async-start(), calls=%async_computation.18 | async-start | bytes 20971520 | tf_op jit(solution)/shard_map/all_gather | solution.py:224
  1052.1 1173.9 %all-gather.22.cloned.1.call-start = ((), (), s32[]{:S(2)}) async-start(), calls=%async_computation.17 | async-start | bytes 2162688 | tf_op jit(solution)/shard_map/all_gather | solution.py:313
  1078.9 1150.9 %all-gather.20.cloned.1.call-start = ((), (), s32[]{:S(2)}) async-start(), calls=%async_computation.15 | async-start | bytes 4325376 | tf_op jit(solution)/shard_map/all_gather | solution.py:310
  1362.2 930.3 %reduce-scatter.5.cloned.1.call-start = ((), (), s32[]{:S(2)}) async-start(), calls=%async_computation.11 | async-start | bytes 9437184 | tf_op jit(solution)/shard_map/reduce_scatter | solution.py:290
  2202.9 126.1 %reduce-scatter.7.cloned.1.call-start = ((), (), s32[]{:S(2)}) async-start(), calls=%async_computation.13 | async-start | bytes 2359296 | tf_op jit(solution)/shard_map/reduce_scatter | solution.py:293
  2211.2 223.4 %all-reduce.125.cloned.1.call-start = ((), (), s32[]{:S(2)}) async-start(), calls=%async_computation.10 | async-start | bytes 8388608 | tf_op jit(solution)/shard_map/psum | solution.py:285
  2225.4 256.8 %all-gather.18.cloned.1.call-start = ((), (), s32[]{:S(2)}) async-start(), calls=%async_computation.12 | async-start | bytes 3145728 | tf_op jit(solution)/shard_map/all_gather | solution.py:304
  (201 other events, 1858.8 us)
Sparse Core Ops, SparseCore 0:
  10.5 152.3 all-gather.9
  164.4 44.1 all-gather.11
  494.9 170.3 all-reduce.120
  667.3 201.7 all-gather.13
  870.6 104.8 all-gather.15
  1002.3 63.0 reduce-scatter.10
  1069.4 170.4 all-reduce.122
  1242.2 119.9 reduce-scatter.8
  1364.6 155.7 all-gather.23
  1521.8 9.4 all-gather.21
  1532.9 12.9 all-gather.19
  2203.1 89.4 reduce-scatter.4
  2294.8 34.1 reduce-scatter.6
  2332.1 102.4 all-reduce.124
  2436.1 10.5 all-gather.17
